TPU v7x, 32 devices: a whole 2x2x4 slice. The times are simulated.
32 devices in a mesh: dp: 2 (over x), ep: 16 (over z, y, core).
Axes of the slice: x: 2, y: 2, z: 4, core: 2. Of those that a mesh axis runs over, the one named last changes fastest.
Arguments:
- queries: bfloat16 [2048, 36864], P('ep', 'dp'), may hold values from -40 to 40
- suffix_latent: bfloat16 [2048, 576], P('ep'), may hold values from -10 to 10
- page_pool: bfloat16 [128, 36864], P('ep'), may hold values from -6 to 6
- page_owner: int32 [16, 32], P('ep'), may hold values from 0 to 15, as said below
- page_slot: int32 [16, 32], P('ep'), may hold values from 0 to 7
- prefix_len: int32 [16], P('ep'), may hold values from 1025 to 2048, as said below
- moe_input: bfloat16 [512, 3584], P(('dp', 'ep')), may hold values from -6 to 6
- expert_ids: int32 [512, 8], P(('dp', 'ep')), may hold values from 0 to 15, all different within a row; in each aligned block of 16 rows (0 to 15, 16 to 31, ...) at most 10 rows name the same one
- gate_weights: float32 [512, 8], P(('dp', 'ep')), may hold values from 0.1 to 0.6
- w_gate: bfloat16 [16, 3584, 1024], P('ep', None, 'dp'), may hold values from -0.09375 to 0.09375
- w_up: bfloat16 [16, 3584, 1024], P('ep', None, 'dp'), may hold values from -0.09375 to 0.09375
- w_down: bfloat16 [16, 1024, 3584], P('ep', 'dp'), may hold values from -0.1875 to 0.1875
Outputs:
- attn_context: bfloat16 [2048, 32768], P('ep', 'dp')
- moe_output: bfloat16 [512, 3584], P(('dp', 'ep'))
Inputs may be any that keep to these rules, and one draw needn't show every extreme that they name: `page_owner`: for a multiple m of the ep axis's size, the pages m, m + 1, ... of one request up to m + that size - 1 have distinct owners, so page k is the (k div that size)-th page of its request on its owner; entries past a request's prefix are valid page references too. `prefix_len`: some request has the longest prefix, 2048 tokens. `expert_ids`: in the 16 rows of one device no expert is named by more than 10 rows.
All inputs are finite; a program needn't handle non-finite values.
Results may differ from a plain program's by a relative error of at most 0.0057.
Values may be sent and summed in bfloat16 or wider, within the bound.
No kernel may reach another device: no remote copies, remote signals or barrier semaphores. Data moves between devices by JAX's collectives and lax.ppermute only.
A program may use at most 192 MiB of HBM per device.

v0:
```python
import jax
import jax.numpy as jnp
from jax import lax
from jax.sharding import PartitionSpec as P

LATENT = 512
ROPE = 64
PAGE = 64
score_scale = 0.07216878364870322
neg_large = -1e30


def attend(query_rows, suffix_rows, prefix_keys, length):
    new_tokens = suffix_rows.shape[0]
    key_width = suffix_rows.shape[1]
    head_count = query_rows.shape[1] // key_width
    flat_queries = query_rows.reshape(new_tokens * head_count, key_width)
    all_keys = jnp.concatenate([prefix_keys, suffix_rows], axis=0)
    scores = (
        lax.dot_general(
            flat_queries, all_keys, (((1,), (1,)), ((), ())), preferred_element_type=jnp.float32
        )
        * score_scale
    )
    prefix_count = prefix_keys.shape[0]
    key_index = jnp.arange(prefix_count + new_tokens, dtype=jnp.int32)[None, :]
    row_token = (jnp.arange(new_tokens * head_count, dtype=jnp.int32) // head_count)[:, None]
    allowed = jnp.where(
        key_index < prefix_count, key_index < length, key_index - prefix_count <= row_token
    )
    masked = jnp.where(allowed, scores, neg_large)
    row_max = jnp.max(masked, axis=1, keepdims=True)
    exponent = jnp.where(allowed, jnp.exp(masked - row_max), 0.0)
    probs = (exponent / jnp.sum(exponent, axis=1, keepdims=True)).astype(jnp.bfloat16)
    context = jnp.dot(probs, all_keys[:, :LATENT], preferred_element_type=jnp.float32)
    return context.astype(jnp.bfloat16).reshape(new_tokens, head_count * LATENT)


def slot_table(owners, slot_ids, targets, slot_count, stride):
    page_rank = jnp.arange(owners.shape[1], dtype=jnp.int32) // stride
    slot_range = jnp.arange(slot_count, dtype=jnp.int32)
    matches = (owners[:, None, None, :] == targets[None, :, None, None]) & (
        page_rank[None, None, None, :] == slot_range[None, None, :, None]
    )
    return jnp.sum(jnp.where(matches, slot_ids[:, None, None, :], 0), axis=3)


def fetch_pages(page_pool, page_owner, page_slot):
    ep_size = lax.axis_size("ep")
    page_total = page_owner.shape[1]
    slot_count = (page_total + ep_size - 1) // ep_size
    everyone = jnp.arange(ep_size, dtype=jnp.int32)
    wanted = slot_table(page_owner, page_slot, everyone, slot_count, ep_size)[0]
    fetched = lax.all_to_all(
        page_pool[lax.all_to_all(wanted, "ep", split_axis=0, concat_axis=0, tiled=True)],
        "ep",
        split_axis=0,
        concat_axis=0,
        tiled=True,
    )
    flat_rows = fetched.reshape(ep_size * slot_count, fetched.shape[2])
    page_order = page_owner[0] * slot_count + jnp.arange(page_total, dtype=jnp.int32) // ep_size
    return flat_rows[page_order].reshape(page_total * PAGE, LATENT + ROPE)


def experts_part(moe_input, expert_ids, gate_weights, w_gate, w_up, w_down):
    ep_size = lax.axis_size("ep")
    tok_count, top_count = expert_ids.shape
    capacity = min(tok_count, max(2, 5 * tok_count * top_count // (4 * ep_size)))
    features = moe_input.shape[1]
    flat_ids = expert_ids.reshape(tok_count * top_count)
    onehot = (flat_ids[:, None] == jnp.arange(ep_size, dtype=jnp.int32)[None, :]).astype(jnp.int32)
    slot_index = jnp.sum((jnp.cumsum(onehot, axis=0) - 1) * onehot, axis=1)
    target = (flat_ids * capacity + slot_index).reshape(tok_count, top_count)
    cells = jnp.arange(ep_size * capacity, dtype=jnp.int32)
    placed = jnp.any(target[None, :, :] == cells[:, None, None], axis=2).astype(jnp.bfloat16)
    outgoing = jnp.dot(placed, moe_input, preferred_element_type=jnp.float32).astype(jnp.bfloat16)
    incoming = lax.all_to_all(
        outgoing.reshape(ep_size, capacity, features), "ep", split_axis=0, concat_axis=0, tiled=True
    )
    incoming = incoming.reshape(ep_size * capacity, features)
    gate_local = w_gate[0]
    up_local = w_up[0]
    down_local = w_down[0]
    shard_part = lax.all_gather(incoming, "dp", axis=0, tiled=True)
    gate_proj = jnp.dot(shard_part, gate_local, preferred_element_type=jnp.float32)
    up_proj = jnp.dot(shard_part, up_local, preferred_element_type=jnp.float32)
    hidden_all = (jax.nn.silu(gate_proj) * up_proj).astype(jnp.bfloat16)
    result = lax.psum_scatter(
        jnp.dot(hidden_all, down_local, preferred_element_type=jnp.float32),
        "dp",
        scatter_dimension=0,
        tiled=True,
    )
    returned = lax.all_to_all(
        result.astype(jnp.bfloat16).reshape(ep_size, capacity, features),
        "ep",
        split_axis=0,
        concat_axis=0,
        tiled=True,
    )
    returned = returned.reshape(ep_size * capacity, features)
    picked = returned[target].astype(jnp.float32)
    return jnp.sum(picked * gate_weights[:, :, None], axis=1).astype(jnp.bfloat16)


def on_device(
    queries,
    suffix_latent,
    page_pool,
    page_owner,
    page_slot,
    prefix_len,
    moe_input,
    expert_ids,
    gate_weights,
    w_gate,
    w_up,
    w_down,
):
    prefix_keys = fetch_pages(page_pool, page_owner, page_slot)
    moe_output = experts_part(moe_input, expert_ids, gate_weights, w_gate, w_up, w_down)
    attn_context = attend(queries, suffix_latent, prefix_keys, prefix_len[0])
    return (attn_context, moe_output)


def solution(mesh):
    return jax.shard_map(
        on_device,
        mesh=mesh,
        in_specs=(
            P("ep", "dp"),
            P("ep", None),
            P("ep", None),
            P("ep", None),
            P("ep", None),
            P("ep"),
            P(("dp", "ep"), None),
            P(("dp", "ep"), None),
            P(("dp", "ep"), None),
            P("ep", None, "dp"),
            P("ep", None, "dp"),
            P("ep", "dp", None),
        ),
        out_specs=(P("ep", "dp"), P(("dp", "ep"), None)),
        check_vma=False,
    )
```

profile of v0, /device:TPU:15, one launch (start us, length us, event | category | flops | bytes accessed | tf_op | source)
XLA Modules:
  0.0 267.8 jit_solution(14442339165964018494)
XLA Ops:
  8.8 2.4 convolution_convert_fusion
  11.2 1.5 reshape.242
  12.7 48.1 %all_to_all.27 = bf16[16,10,3584]{2,1,0:T(8,128)(2,1)} all-to-all(bf16[16,10,3584]{2,1,0:T(8,128)(2,1)S(1)} %reshape.242), channel_id=1, replica_groups=mesh['dp'=2,'ep'=16] {'ep'}, dimensions={0} | all-to-all | bytes 2293760 | tf_op jit(solution)/shard_map/all_to_all | solution.py:78
  60.8 2.5 reshape.243
  63.5 8.6 %all_to_all.28 = s32[16,1,2]{2,1,0:T(1,128)S(1)} all-to-all(s32[16,1,2]{2,1,0:T(1,128)S(1)} %copy.31), channel_id=1, replica_groups=mesh['dp'=2,'ep'=16] {'ep'}, dimensions={0} | all-to-all | bytes 256 | tf_op jit(solution)/shard_map/all_to_all | solution.py:55
  72.5 2.1 gather_fusion
  74.6 2.8 %reshape.247 = bf16[16,2,36864]{2,1,0:T(2,128)(2,1)} reshape(bf16[32,36864]{1,0:T(8,128)(2,1)S(1)} %gather_fusion) | data formatting | bytes 4718592 | tf_op jit(solution)/shard_map/gather | solution.py:55
  77.4 6.9 %all-to-all-start.1 = ((bf16[16,2,36864]{2,1,0:T(2,128)(2,1)}), bf16[16,2,36864]{2,1,0:T(2,128)(2,1)}, u32[]{:S(2)}, u32[]{:S(2)}) async-start(bf16[16,2,36864]{2,1,0:T(2,128)(2,1)} %reshape.247), calls=%async_computation.1 | async-start | bytes 4718592 | tf_op jit(solution)/shard_map/all_to_all | solution.py:54
  84.3 13.0 %all-gather.2.cloned.1.call-done = bf16[320,3584]{1,0:T(8,128)(2,1)} async-done(((bf16[160,3584]{1,0:T(8,128)(2,1)}), bf16[320,3584]{1,0:T(8,128)(2,1)}) %all-gather.2.cloned.1.call-update) | async-done | bytes 2293776 | tf_op jit(solution)/shard_map/all_gather | solution.py:85
  97.3 5.1 %fusion.7 = f32[320,512]{1,0:T(8,128)} fusion(bf16[320,3584]{1,0:T(8,128)(2,1)} %all-gather.2.cloned.1.call-done, bf16[1,3584,512]{2,1,0:T(8,128)(2,1)} %param.21), kind=kOutput, calls=%fused_computation.15 | convolution fusion | flops 1174405120 | bytes 6619136 | tf_op jit(solution)/shard_map/dot_general | solution.py:86
  102.3 8.1 %fusion.3 = f32[320,3584]{1,0:T(8,128)} fusion(bf16[1,512,3584]{2,1,0:T(8,128)(2,1)} %param.23, bf16[320,3584]{1,0:T(8,128)(2,1)S(1)} %copy-done.8, bf16[1,3584,512]{2,1,0:T(8,128)(2,1)} %param.22, f32[320,512]{1,0:T(8,128)} %fusion.7), kind=kOutput, calls=%fused_computation.11 | convolution fusion | flops 2349793280 | bytes 14876672 | tf_op jit(solution)/shard_map/dot_general | solution.py:90
  111.5 10.1 %reshape.240 = bf16[4096,576]{1,0:T(8,128)(2,1)} reshape(bf16[128,18432]{1,0:T(8,128)(2,1)} %param.12) | data formatting | bytes 9437184 | tf_op jit(solution)/shard_map/reshape | solution.py:17
  121.8 15.8 %all-to-all-done.1 = bf16[16,2,36864]{2,1,0:T(2,128)(2,1)} async-done(((bf16[16,2,36864]{2,1,0:T(2,128)(2,1)}), bf16[16,2,36864]{2,1,0:T(2,128)(2,1)}, u32[]{:S(2)}, u32[]{:S(2)}) %all-to-all-start.1) | async-done | bytes 2359328 | tf_op jit(solution)/shard_map/all_to_all | solution.py:54
  137.7 3.0 %reshape.238 = bf16[32,36864]{1,0:T(8,128)(2,1)S(1)} reshape(bf16[16,2,36864]{2,1,0:T(2,128)(2,1)} %all-to-all-done.1) | data formatting | bytes 4718592 | tf_op jit(solution)/shard_map/reshape | solution.py:61
  140.7 3.5 %gather_fusion.1 = bf16[32,36864]{1,0:T(8,128)(2,1)} fusion(bf16[32,36864]{1,0:T(8,128)(2,1)S(1)} %reshape.238, s32[1024]{0:T(1024)S(1)} %pad_clamp_fusion.1), kind=kCustom, calls=%fused_computation.1 | custom fusion | bytes 4718720 | tf_op jit(solution)/shard_map/gather | solution.py:63
  144.2 4.6 %reshape.239 = bf16[2048,576]{1,0:T(8,128)(2,1)S(1)} reshape(bf16[32,36864]{1,0:T(8,128)(2,1)} %gather_fusion.1) | data formatting | bytes 4718592 | tf_op jit(solution)/shard_map/reshape | solution.py:63
  148.8 25.5 %fusion = (f32[4096]{0:T(1024)S(1)}, f32[2176,4096]{1,0:T(8,128)}) fusion(s32[4096]{0:T(1024)S(1)} %add_select_fusion, s32[2176]{0:T(1024)S(1)} %iota_add_fusion, pred[2176]{0:T(1024)(128)(4,1)S(1)} %get-tuple-element.8, pred[2176]{0:T(1024)(128)(4,1)S(1)} %get-tuple-element.9, bf16[4096,576]{1,0:T(8,128)(2,1)} %reshape.240, bf16[128,576]{1,0:T(8,128)(2,1)S(1)} %copy.34, ...), kind=kOutput, calls=%fused_computation.7 | convolution fusion | flops 10317230080 | bytes 42922752 | tf_op jit(solution)/shard_map/dot_general | solution.py:20
  174.3 32.7 %fusion.41 = (f32[4096]{0:T(1024)S(1)}, f32[4096,2176]{0,1:T(8,128)}) fusion(f32[4096]{0:T(1024)S(1)} %get-tuple-element.6, f32[2176,4096]{1,0:T(8,128)} %get-tuple-element.7, s32[4096]{0:T(1024)S(1)} %add_select_fusion, s32[2176]{0:T(1024)S(1)} %iota_add_fusion, pred[2176]{0:T(1024)(128)(4,1)S(1)} %get-tuple-element.8, pred[2176]{0:T(1024)(128)(4,1)S(1)} %get-tuple-element.9), kind=kLoop, calls=%fused_computation.72 | loop fusion | flops 62386176 | bytes 71365376 | tf_op jit(solution)/shard_map/reduce_sum | solution.py:34
  207.0 1.8 convert_element_type.30
  210.2 4.8 %all-to-all-start.3 = ((bf16[16,10,3584]{2,1,0:T(8,128)(2,1)}), bf16[16,10,3584]{2,1,0:T(8,128)(2,1)}, u32[]{:S(2)}, u32[]{:S(2)}) async-start(bf16[16,10,3584]{2,1,0:T(8,128)(2,1)} %reshape.244), calls=%async_computation.4 | async-start | bytes 3670016 | tf_op jit(solution)/shard_map/all_to_all | solution.py:95
  215.0 17.7 %fusion.2 = bf16[4096,512]{1,0:T(8,128)(2,1)} fusion(f32[4096,2176]{0,1:T(8,128)} %get-tuple-element.5, f32[4096]{0:T(1024)S(1)} %get-tuple-element.4, bf16[128,576]{1,0:T(8,128)(2,1)S(1)} %copy.34, bf16[2048,576]{1,0:T(8,128)(2,1)S(1)} %copy-done.3), kind=kOutput, calls=%fused_computation.9 | convolution fusion | flops 9151184896 | bytes 42369024 | tf_op jit(solution)/shard_map/dot_general | solution.py:35
  232.7 7.4 %reshape.241 = bf16[128,16384]{1,0:T(8,128)(2,1)} reshape(bf16[4096,512]{1,0:T(8,128)(2,1)} %fusion.2) | data formatting | bytes 8388608 | tf_op jit(solution)/shard_map/reshape | solution.py:36
  240.1 16.6 %all-to-all-done.3 = bf16[16,10,3584]{2,1,0:T(8,128)(2,1)} async-done(((bf16[16,10,3584]{2,1,0:T(8,128)(2,1)}), bf16[16,10,3584]{2,1,0:T(8,128)(2,1)}, u32[]{:S(2)}, u32[]{:S(2)}) %all-to-all-start.3) | async-done | bytes 1146912 | tf_op jit(solution)/shard_map/all_to_all | solution.py:95
  256.7 1.7 reshape.245
  (53 shorter events, 6.7 us)
Async XLA Ops:
  7.2 65.3 %copy-start = (bf16[8,36864]{1,0:T(8,128)(2,1)S(1)}, bf16[8,36864]{1,0:T(8,128)(2,1)}, u32[]{:S(2)}) copy-start(bf16[8,36864]{1,0:T(8,128)(2,1)} %param.14) | copy-start | bytes 1769476
  7.2 90.1 %all-gather.2.cloned.1.call-start = ((), (), s32[]{:S(2)}) async-start(), calls=%async_computation.5 | async-start | bytes 3440640 | tf_op jit(solution)/shard_map/all_gather | solution.py:85
  12.7 50.6 %copy-start.6 = (s32[1,32]{1,0:T(1,128)S(1)}, s32[1,32]{1,0:T(1,128)}, u32[]{:S(2)}) copy-start(s32[1,32]{1,0:T(1,128)} %param.15) | copy-start | bytes 388
  12.7 50.6 %copy-start.7 = (s32[1,32]{1,0:T(1,128)S(1)}, s32[1,32]{1,0:T(1,128)}, u32[]{:S(2)}) copy-start(s32[1,32]{1,0:T(1,128)} %param.16) | copy-start | bytes 388
  77.4 60.3 %all-to-all-start.1 = ((bf16[16,2,36864]{2,1,0:T(2,128)(2,1)}), bf16[16,2,36864]{2,1,0:T(2,128)(2,1)}, u32[]{:S(2)}, u32[]{:S(2)}) async-start(bf16[16,2,36864]{2,1,0:T(2,128)(2,1)} %reshape.247), calls=%async_computation.1 | async-start | bytes 4718592 | tf_op jit(solution)/shard_map/all_to_all | solution.py:54
  84.2 122.8 %reduce-scatter.2.cloned.1.call-start = ((), (), s32[]{:S(2)}) async-start(), calls=%async_computation.6 | async-start | bytes 6881280 | tf_op jit(solution)/shard_map/reduce_scatter | solution.py:89
  97.3 5.1 %copy-start.8 = (bf16[320,3584]{1,0:T(8,128)(2,1)S(1)}, bf16[320,3584]{1,0:T(8,128)(2,1)}, u32[]{:S(2)}) copy-start(bf16[320,3584]{1,0:T(8,128)(2,1)} %all-gather.2.cloned.1.call-done) | copy-start | bytes 6881284
  110.4 0.9 copy-start.4
  111.5 10.2 %copy-start.5 = (f32[16,8]{0,1:T(8,128)S(1)}, f32[16,8]{0,1:T(8,128)}, u32[]{:S(2)}) copy-start(f32[16,8]{0,1:T(8,128)} %param.20) | copy-start | bytes 1540
  148.8 25.5 %copy-start.2 = (bf16[2048,576]{1,0:T(8,128)(2,1)}, bf16[2048,576]{1,0:T(8,128)(2,1)S(1)}, u32[]{:S(2)}) copy-start(bf16[2048,576]{1,0:T(8,128)(2,1)S(1)} %reshape.239) | copy-start | bytes 7077892
  210.2 4.8 %copy-start.3 = (bf16[2048,576]{1,0:T(8,128)(2,1)S(1)}, bf16[2048,576]{1,0:T(8,128)(2,1)}, u32[]{:S(2)}) copy-start(bf16[2048,576]{1,0:T(8,128)(2,1)} %copy-done.2) | copy-start | bytes 7077892
  210.2 46.5 %all-to-all-start.3 = ((bf16[16,10,3584]{2,1,0:T(8,128)(2,1)}), bf16[16,10,3584]{2,1,0:T(8,128)(2,1)}, u32[]{:S(2)}, u32[]{:S(2)}) async-start(bf16[16,10,3584]{2,1,0:T(8,128)(2,1)} %reshape.244), calls=%async_computation.4 | async-start | bytes 3670016 | tf_op jit(solution)/shard_map/all_to_all | solution.py:95
  256.7 4.2 %copy-start.1 = (bf16[8,36864]{1,0:T(8,128)(2,1)S(1)}, bf16[8,36864]{1,0:T(8,128)(2,1)}, u32[]{:S(2)}) copy-start(bf16[8,36864]{1,0:T(8,128)(2,1)} %param.14) | copy-start | bytes 1769476
Sparse Core Ops, SparseCore 0:
  63.4 33.8 all-gather.1
  110.6 58.6 reduce-scatter.1
where the time goes:
time: 269 us; the launch traced here: 268 us
  matrix products  58.7 us (22%)
  blocking collectives  56.7 us (21%)
  waiting for transfers between devices  45.5 us (17%)
  local copies, waits for them, and re-layouts  43.5 us (16%)
  other arithmetic  36.6 us (14%)
  between operations  15 us (6%)
  starting transfers between devices  11.8 us (4%)
    all_to_all x1, blocking collectives, experts_part(): lax.all_to_all(outgoing.reshape(ep_size, capacity, features), 'ep', split...  48.1 us
    reduce_sum x1, other arithmetic, attend(): jnp.sum(exponent, axis=1, keepdims=True)  32.7 us
    dot_general x1, matrix products, attend(): lax.dot_general(flat_queries, all_keys, (((1,), (1,)), ((), ())), preferr...  25.5 us
    dot_general x1, matrix products, attend(): jnp.dot(probs, all_keys[:, :LATENT], preferred_element_type=jnp.float32)  17.7 us
    all_to_all x1, waiting for transfers between devices, experts_part(): lax.all_to_all(result.astype(jnp.bfloat16).reshape(ep_size, capacity, fea...  16.6 us
    all_to_all x1, waiting for transfers between devices, fetch_pages(): lax.all_to_all(page_pool[lax.all_to_all(wanted, 'ep', split_axis=0, conca...  15.8 us
    all_gather x1, waiting for transfers between devices, experts_part(): shard_part = lax.all_gather(incoming, 'dp', axis=0, tiled=True)  13 us
    reshape x1, local copies, waits for them, and re-layouts, attend(): flat_queries = query_rows.reshape(new_tokens * head_count, key_width)  10.1 us
  transfers between devices with their start and end apart: 4, of which 3 were waited for; matrix products, arithmetic and copies ran while one was open for 46% of the time, Pallas kernels for 0%

commit v1 on v0

--- a/solution.py
+++ b/solution.py
@@ -51,13 +51,20 @@
     slot_count = (page_total + ep_size - 1) // ep_size
     everyone = jnp.arange(ep_size, dtype=jnp.int32)
     wanted = slot_table(page_owner, page_slot, everyone, slot_count, ep_size)[0]
-    fetched = lax.all_to_all(
-        page_pool[lax.all_to_all(wanted, "ep", split_axis=0, concat_axis=0, tiled=True)],
-        "ep",
-        split_axis=0,
-        concat_axis=0,
-        tiled=True,
-    )
+    shard = page_pool[lax.all_to_all(wanted, "ep", split_axis=0, concat_axis=0, tiled=True)]
+    ways, here = (lax.axis_size("ep"), lax.axis_index("ep"))
+    width = shard.shape[0] // ways
+    shape = list(shard.shape)
+    shape[0] = width
+    height = shape[0]
+    shape[0] = height * ways
+    full = jnp.zeros(shape, shard.dtype)
+    for mask in range(ways):
+        part = lax.dynamic_slice_in_dim(shard, (here ^ mask) * width, width, axis=0)
+        if mask:
+            part = lax.ppermute(part, "ep", [(d, d ^ mask) for d in range(ways)])
+        full = lax.dynamic_update_slice_in_dim(full, part, (here ^ mask) * height, axis=0)
+    fetched = full
     flat_rows = fetched.reshape(ep_size * slot_count, fetched.shape[2])
     page_order = page_owner[0] * slot_count + jnp.arange(page_total, dtype=jnp.int32) // ep_size
     return flat_rows[page_order].reshape(page_total * PAGE, LATENT + ROPE)

time: 269 us -> 299 us (1.11)
  blocking collectives: 56.7 us -> 0 us
  waiting for transfers between devices: 45.5 us -> 83.7 us
  starting transfers between devices: 11.8 us -> 41.3 us
  local copies, waits for them, and re-layouts: 43.5 us -> 61.2 us
    all_to_all x2 -> x0, blocking collectives: 56.7 us -> none  [the longest x1 48.1 us: experts_part(): lax.all_to_all(outgoing.reshape(ep_size, capacity, features), 'ep', split...]
    ppermute x0 -> x15, waiting for transfers between devices: none -> 34.3 us  [fetch_pages(): part = lax.ppermute(part, 'ep', [(d, d ^ mask) for d in range(ways)])]
    ppermute x0 -> x15, starting transfers between devices: none -> 21.8 us  [fetch_pages(): part = lax.ppermute(part, 'ep', [(d, d ^ mask) for d in range(ways)])]
    all_gather x1, waiting for transfers between devices: 13 us -> 32.5 us  [experts_part(): shard_part = lax.all_gather(incoming, 'dp', axis=0, tiled=True)]
    all_to_all x1 -> x2, waiting for transfers between devices: 15.8 us -> 0.01 us  [the longest x1 0.01 us: fetch_pages(): lax.all_to_all(wanted, 'ep', split_axis=0, concat_axis=0, tiled=True)]
    dynamic_update_slice x0 -> x15, local copies, waits for them, and re-layouts: none -> 11.5 us  [fetch_pages(): lax.dynamic_update_slice_in_dim(full, part, (here ^ mask) * height, axis=0)]
    all_to_all x1 -> x2, starting transfers between devices: 6.88 us -> 12.6 us  [the longest x1 6.52 us: fetch_pages(): lax.all_to_all(wanted, 'ep', split_axis=0, concat_axis=0, tiled=True)]
    broadcast_in_dim x0 -> x1, local copies, waits for them, and re-layouts: none -> 3.23 us  [fetch_pages(): full = jnp.zeros(shape, shard.dtype)]
  transfers between devices with their start and end apart: 4 -> 20, of which waited for: 3 -> 9; matrix products, arithmetic and copies ran while one was open for 46% -> 50% of each run, Pallas kernels for 0% -> 0%
where the time goes in v1:
time: 299 us; the launch traced here: 297 us
  waiting for transfers between devices  83.7 us (28%)
  local copies, waits for them, and re-layouts  61.2 us (20%)
  matrix products  57.2 us (19%)
  starting transfers between devices  41.3 us (14%)
  other arithmetic  38.6 us (13%)
  between operations  15 us (5%)
    ppermute x15, waiting for transfers between devices, fetch_pages(): part = lax.ppermute(part, 'ep', [(d, d ^ mask) for d in range(ways)])  34.3 us
    reduce_sum x1, other arithmetic, attend(): jnp.sum(exponent, axis=1, keepdims=True)  32.7 us
    all_gather x1, waiting for transfers between devices, experts_part(): shard_part = lax.all_gather(incoming, 'dp', axis=0, tiled=True)  32.5 us
    dot_general x1, matrix products, attend(): lax.dot_general(flat_queries, all_keys, (((1,), (1,)), ((), ())), preferr...  25.5 us
    ppermute x15, starting transfers between devices, fetch_pages(): part = lax.ppermute(part, 'ep', [(d, d ^ mask) for d in range(ways)])  21.8 us
    dot_general x1, matrix products, attend(): jnp.dot(probs, all_keys[:, :LATENT], preferred_element_type=jnp.float32)  17.7 us
    all_to_all x1, waiting for transfers between devices, experts_part(): lax.all_to_all(result.astype(jnp.bfloat16).reshape(ep_size, capacity, fea...  16.9 us
    dynamic_update_slice x15, local copies, waits for them, and re-layouts, fetch_pages(): lax.dynamic_update_slice_in_dim(full, part, (here ^ mask) * height, axis=0)  11.5 us
  transfers between devices with their start and end apart: 20, of which 9 were waited for; matrix products, arithmetic and copies ran while one was open for 50% of the time, Pallas kernels for 0%

profile of v1, /device:TPU:15, one launch (start us, length us, event | category | flops | bytes accessed | tf_op | source)
XLA Modules:
  0.0 297.0 jit_solution(3773336234411104104)
XLA Ops:
  9.4 6.5 %all-to-all-start = ((s32[16,1,2]{2,1,0:T(1,128)}), s32[16,1,2]{2,1,0:T(1,128)S(1)}, u32[]{:S(2)}, u32[]{:S(2)}) async-start(s32[16,1,2]{2,1,0:T(1,128)} %copy.31), calls=%async_computation | async-start | bytes 16384 | tf_op jit(solution)/shard_map/all_to_all | solution.py:54
  21.8 6.0 %all-to-all-start.1 = ((bf16[16,10,3584]{2,1,0:T(8,128)(2,1)}), bf16[16,10,3584]{2,1,0:T(8,128)(2,1)}, u32[]{:S(2)}, u32[]{:S(2)}) async-start(bf16[16,10,3584]{2,1,0:T(8,128)(2,1)} %reshape.242), calls=%async_computation.1 | async-start | bytes 3670016 | tf_op jit(solution)/shard_map/all_to_all | solution.py:85
  33.1 3.2 %broadcast_in_dim.59 = bf16[16,2,36864]{2,1,0:T(2,128)(2,1)} broadcast(bf16[]{:T(256)} %constant.40.clone.1), dimensions={} | broadcast | bytes 2359298 | tf_op jit(solution)/shard_map/broadcast_in_dim | solution.py:61
  36.3 3.0 constant_dynamic-slice_fusion
  39.9 9.8 %reshape.240 = bf16[4096,576]{1,0:T(8,128)(2,1)} reshape(bf16[128,18432]{1,0:T(8,128)(2,1)} %param.12) | data formatting | bytes 9437184 | tf_op jit(solution)/shard_map/reshape | solution.py:17
  54.1 4.0 %collective-permute-done.1 = bf16[1,2,36864]{2,1,0:T(2,128)(2,1)S(1)} collective-permute-done((bf16[1,2,36864]{2,1,0:T(2,128)(2,1)S(1)}, bf16[1,2,36864]{2,1,0:T(2,128)(2,1)S(1)}, u32[]{:S(2)}, u32[]{:S(2)}) %collective-permute-start.1) | collective-permute-done | bytes 147488 | tf_op jit(solution)/shard_map/ppermute | solution.py:65
  58.9 4.8 %collective-permute-done.2 = bf16[1,2,36864]{2,1,0:T(2,128)(2,1)S(1)} collective-permute-done((bf16[1,2,36864]{2,1,0:T(2,128)(2,1)S(1)}, bf16[1,2,36864]{2,1,0:T(2,128)(2,1)S(1)}, u32[]{:S(2)}, u32[]{:S(2)}) %collective-permute-start.2) | collective-permute-done | bytes 147488 | tf_op jit(solution)/shard_map/ppermute | solution.py:65
  67.6 10.4 %collective-permute-start.9 = (bf16[1,2,36864]{2,1,0:T(2,128)(2,1)S(1)}, bf16[1,2,36864]{2,1,0:T(2,128)(2,1)S(1)}, u32[]{:S(2)}, u32[]{:S(2)}) collective-permute-start(bf16[1,2,36864]{2,1,0:T(2,128)(2,1)S(1)} %get-tuple-element.11), channel_id=1, source_target_pairs={{0,10},{1,11},{2,8},{3,9},{4,14},{5,15},{6,12},{7,13},{8,2},{9,3},... | collective-permute-start | bytes 442376 | tf_op jit(solution)/shard_map/ppermute | solution.py:65
  83.1 10.1 %collective-permute-done.8 = bf16[1,2,36864]{2,1,0:T(2,128)(2,1)S(1)} collective-permute-done((bf16[1,2,36864]{2,1,0:T(2,128)(2,1)S(1)}, bf16[1,2,36864]{2,1,0:T(2,128)(2,1)S(1)}, u32[]{:S(2)}, u32[]{:S(2)}) %collective-permute-start.8) | collective-permute-done | bytes 147488 | tf_op jit(solution)/shard_map/ppermute | solution.py:65
  96.3 3.0 %collective-permute-start.14 = (bf16[1,2,36864]{2,1,0:T(2,128)(2,1)S(1)}, bf16[1,2,36864]{2,1,0:T(2,128)(2,1)S(1)}, u32[]{:S(2)}, u32[]{:S(2)}) collective-permute-start(bf16[1,2,36864]{2,1,0:T(2,128)(2,1)S(1)} %get-tuple-element.6), channel_id=1, source_target_pairs={{0,15},{1,14},{2,13},{3,12},{4,11},{5,10},{6,9},{7,8},{8,7},{9,6},... | collective-permute-start | bytes 442376 | tf_op jit(solution)/shard_map/ppermute | solution.py:65
  103.4 7.2 %collective-permute-done.11 = bf16[1,2,36864]{2,1,0:T(2,128)(2,1)S(1)} collective-permute-done((bf16[1,2,36864]{2,1,0:T(2,128)(2,1)S(1)}, bf16[1,2,36864]{2,1,0:T(2,128)(2,1)S(1)}, u32[]{:S(2)}, u32[]{:S(2)}) %collective-permute-start.11) | collective-permute-done | bytes 147488 | tf_op jit(solution)/shard_map/ppermute | solution.py:65
  111.4 3.2 %collective-permute-done.12 = bf16[1,2,36864]{2,1,0:T(2,128)(2,1)S(1)} collective-permute-done((bf16[1,2,36864]{2,1,0:T(2,128)(2,1)S(1)}, bf16[1,2,36864]{2,1,0:T(2,128)(2,1)S(1)}, u32[]{:S(2)}, u32[]{:S(2)}) %collective-permute-start.12) | collective-permute-done | bytes 147488 | tf_op jit(solution)/shard_map/ppermute | solution.py:65
  118.9 32.5 %all-gather.2.cloned.1.call-done = bf16[320,3584]{1,0:T(8,128)(2,1)} async-done(((bf16[160,3584]{1,0:T(8,128)(2,1)}), bf16[320,3584]{1,0:T(8,128)(2,1)}) %all-gather.2.cloned.1.call-update) | async-done | bytes 2293776 | tf_op jit(solution)/shard_map/all_gather | solution.py:92
  151.4 4.1 %fusion.7 = f32[320,512]{1,0:T(8,128)S(1)} fusion(bf16[320,3584]{1,0:T(8,128)(2,1)} %all-gather.2.cloned.1.call-done, bf16[1,3584,512]{2,1,0:T(8,128)(2,1)} %param.21), kind=kOutput, calls=%fused_computation.15 | convolution fusion | flops 1174405120 | bytes 6619136 | tf_op jit(solution)/shard_map/dot_general | solution.py:93
  155.5 8.6 %fusion.3 = f32[320,3584]{1,0:T(8,128)} fusion(bf16[1,512,3584]{2,1,0:T(8,128)(2,1)} %param.23, bf16[320,3584]{1,0:T(8,128)(2,1)} %all-gather.2.cloned.1.call-done, bf16[1,3584,512]{2,1,0:T(8,128)(2,1)} %param.22, f32[320,512]{1,0:T(8,128)S(1)} %fusion.7), kind=kOutput, calls=%fused_computation.11 | convolution fusion | flops 2349793280 | bytes 14876672 | tf_op jit(solution)/shard_map/dot_general | solution.py:97
  164.8 2.9 reshape.238
  167.7 3.5 %gather_fusion.1 = bf16[32,36864]{1,0:T(8,128)(2,1)} fusion(bf16[32,36864]{1,0:T(8,128)(2,1)S(1)} %reshape.238, s32[1024]{0:T(1024)S(1)} %pad_clamp_fusion.1), kind=kCustom, calls=%fused_computation.1 | custom fusion | bytes 4718720 | tf_op jit(solution)/shard_map/gather | solution.py:70
  171.2 4.7 %reshape.239 = bf16[2048,576]{1,0:T(8,128)(2,1)S(1)} reshape(bf16[32,36864]{1,0:T(8,128)(2,1)} %gather_fusion.1) | data formatting | bytes 4718592 | tf_op jit(solution)/shard_map/reshape | solution.py:70
  175.9 25.5 %fusion = (f32[4096]{0:T(1024)S(1)}, f32[2176,4096]{1,0:T(8,128)}) fusion(s32[4096]{0:T(1024)S(1)} %add_select_fusion, s32[2176]{0:T(1024)S(1)} %iota_add_fusion, pred[2176]{0:T(1024)(128)(4,1)S(1)} %get-tuple-element.24, pred[2176]{0:T(1024)(128)(4,1)S(1)} %get-tuple-element.25, bf16[4096,576]{1,0:T(8,128)(2,1)} %reshape.240, ...), kind=kOutput, calls=%fused_computation.7 | convolution fusion | flops 10317230080 | bytes 42922752 | tf_op jit(solution)/shard_map/dot_general | solution.py:20
  201.4 32.7 %fusion.41 = (f32[4096]{0:T(1024)S(1)}, f32[4096,2176]{0,1:T(8,128)}) fusion(f32[4096]{0:T(1024)S(1)} %get-tuple-element.22, f32[2176,4096]{1,0:T(8,128)} %get-tuple-element.23, s32[4096]{0:T(1024)S(1)} %add_select_fusion, s32[2176]{0:T(1024)S(1)} %iota_add_fusion, pred[2176]{0:T(1024)(128)(4,1)S(1)} %get-tuple-element.24, ...), kind=kLoop, calls=%fused_computation.103 | loop fusion | flops 62386176 | bytes 71365376 | tf_op jit(solution)/shard_map/reduce_sum | solution.py:34
  237.3 6.7 %all-to-all-start.2 = ((bf16[16,10,3584]{2,1,0:T(8,128)(2,1)}), bf16[16,10,3584]{2,1,0:T(8,128)(2,1)}, u32[]{:S(2)}, u32[]{:S(2)}) async-start(bf16[16,10,3584]{2,1,0:T(8,128)(2,1)} %reshape.244), calls=%async_computation.3 | async-start | bytes 3670016 | tf_op jit(solution)/shard_map/all_to_all | solution.py:102
  244.1 17.7 %fusion.2 = bf16[4096,512]{1,0:T(8,128)(2,1)} fusion(f32[4096,2176]{0,1:T(8,128)} %get-tuple-element.5, f32[4096]{0:T(1024)S(1)} %get-tuple-element.4, bf16[128,576]{1,0:T(8,128)(2,1)S(1)} %copy.34, bf16[2048,576]{1,0:T(8,128)(2,1)S(1)} %copy-done.4), kind=kOutput, calls=%fused_computation.9 | convolution fusion | flops 9151184896 | bytes 42369024 | tf_op jit(solution)/shard_map/dot_general | solution.py:35
  261.7 7.4 %reshape.241 = bf16[128,16384]{1,0:T(8,128)(2,1)} reshape(bf16[4096,512]{1,0:T(8,128)(2,1)} %fusion.2) | data formatting | bytes 8388608 | tf_op jit(solution)/shard_map/reshape | solution.py:36
  269.1 16.9 %all-to-all-done.2 = bf16[16,10,3584]{2,1,0:T(8,128)(2,1)} async-done(((bf16[16,10,3584]{2,1,0:T(8,128)(2,1)}), bf16[16,10,3584]{2,1,0:T(8,128)(2,1)}, u32[]{:S(2)}, u32[]{:S(2)}) %all-to-all-start.2) | async-done | bytes 1146912 | tf_op jit(solution)/shard_map/all_to_all | solution.py:102
  (96 shorter events, 47.6 us)
Async XLA Ops:
  7.2 21.0 %copy-start = (bf16[8,36864]{1,0:T(8,128)(2,1)S(1)}, bf16[8,36864]{1,0:T(8,128)(2,1)}, u32[]{:S(2)}) copy-start(bf16[8,36864]{1,0:T(8,128)(2,1)} %param.14) | copy-start | bytes 1769476
  9.4 12.4 %all-to-all-start = ((s32[16,1,2]{2,1,0:T(1,128)}), s32[16,1,2]{2,1,0:T(1,128)S(1)}, u32[]{:S(2)}, u32[]{:S(2)}) async-start(s32[16,1,2]{2,1,0:T(1,128)} %copy.31), calls=%async_computation | async-start | bytes 16384 | tf_op jit(solution)/shard_map/all_to_all | solution.py:54
  21.8 93.6 %all-to-all-start.1 = ((bf16[16,10,3584]{2,1,0:T(8,128)(2,1)}), bf16[16,10,3584]{2,1,0:T(8,128)(2,1)}, u32[]{:S(2)}, u32[]{:S(2)}) async-start(bf16[16,10,3584]{2,1,0:T(8,128)(2,1)} %reshape.242), calls=%async_computation.1 | async-start | bytes 3670016 | tf_op jit(solution)/shard_map/all_to_all | solution.py:85
  27.8 123.5 %all-gather.2.cloned.1.call-start = ((), (), s32[]{:S(2)}) async-start(), calls=%async_computation.4 | async-start | bytes 3440640 | tf_op jit(solution)/shard_map/all_gather | solution.py:92
  39.3 14.0 %collective-permute-start = (bf16[1,2,36864]{2,1,0:T(2,128)(2,1)S(1)}, bf16[1,2,36864]{2,1,0:T(2,128)(2,1)S(1)}, u32[]{:S(2)}, u32[]{:S(2)}) collective-permute-start(bf16[1,2,36864]{2,1,0:T(2,128)(2,1)S(1)} %get-tuple-element.20), channel_id=1, source_target_pairs={{0,1},{1,0},{2,3},{3,2},{4,5},{5,4},{6,7},{7,6},{8,9},{9,8},{10,11... | collective-permute-start | bytes 442376 | tf_op jit(solution)/shard_map/ppermute | solution.py:65
  39.8 9.8 %copy-start.6 = (f32[16,8]{0,1:T(8,128)S(1)}, f32[16,8]{0,1:T(8,128)}, u32[]{:S(2)}) copy-start(f32[16,8]{0,1:T(8,128)} %param.20) | copy-start | bytes 1540
  49.8 8.4 %collective-permute-start.1 = (bf16[1,2,36864]{2,1,0:T(2,128)(2,1)S(1)}, bf16[1,2,36864]{2,1,0:T(2,128)(2,1)S(1)}, u32[]{:S(2)}, u32[]{:S(2)}) collective-permute-start(bf16[1,2,36864]{2,1,0:T(2,128)(2,1)S(1)} %get-tuple-element.19), channel_id=1, source_target_pairs={{0,2},{1,3},{2,0},{3,1},{4,6},{5,7},{6,4},{7,5},{8,10},{9,11},{10,... | collective-permute-start | bytes 442376 | tf_op jit(solution)/shard_map/ppermute | solution.py:65
  50.1 13.7 %collective-permute-start.2 = (bf16[1,2,36864]{2,1,0:T(2,128)(2,1)S(1)}, bf16[1,2,36864]{2,1,0:T(2,128)(2,1)S(1)}, u32[]{:S(2)}, u32[]{:S(2)}) collective-permute-start(bf16[1,2,36864]{2,1,0:T(2,128)(2,1)S(1)} %get-tuple-element.18), channel_id=1, source_target_pairs={{0,3},{1,2},{2,1},{3,0},{4,7},{5,6},{6,5},{7,4},{8,11},{9,10},{10,... | collective-permute-start | bytes 442376 | tf_op jit(solution)/shard_map/ppermute | solution.py:65
  51.5 13.4 %collective-permute-start.3 = (bf16[1,2,36864]{2,1,0:T(2,128)(2,1)S(1)}, bf16[1,2,36864]{2,1,0:T(2,128)(2,1)S(1)}, u32[]{:S(2)}, u32[]{:S(2)}) collective-permute-start(bf16[1,2,36864]{2,1,0:T(2,128)(2,1)S(1)} %get-tuple-element.17), channel_id=1, source_target_pairs={{0,4},{1,5},{2,6},{3,7},{4,0},{5,1},{6,2},{7,3},{8,12},{9,13},{10,... | collective-permute-start | bytes 442376 | tf_op jit(solution)/shard_map/ppermute | solution.py:65
  51.8 15.8 %collective-permute-start.4 = (bf16[1,2,36864]{2,1,0:T(2,128)(2,1)S(1)}, bf16[1,2,36864]{2,1,0:T(2,128)(2,1)S(1)}, u32[]{:S(2)}, u32[]{:S(2)}) collective-permute-start(bf16[1,2,36864]{2,1,0:T(2,128)(2,1)S(1)} %get-tuple-element.16), channel_id=1, source_target_pairs={{0,5},{1,4},{2,7},{3,6},{4,1},{5,0},{6,3},{7,2},{8,13},{9,12},{10,... | collective-permute-start | bytes 442376 | tf_op jit(solution)/shard_map/ppermute | solution.py:65
  53.3 25.5 %collective-permute-start.5 = (bf16[1,2,36864]{2,1,0:T(2,128)(2,1)S(1)}, bf16[1,2,36864]{2,1,0:T(2,128)(2,1)S(1)}, u32[]{:S(2)}, u32[]{:S(2)}) collective-permute-start(bf16[1,2,36864]{2,1,0:T(2,128)(2,1)S(1)} %get-tuple-element.15), channel_id=1, source_target_pairs={{0,6},{1,7},{2,4},{3,5},{4,2},{5,3},{6,0},{7,1},{8,14},{9,15},{10,... | collective-permute-start | bytes 442376 | tf_op jit(solution)/shard_map/ppermute | solution.py:65
  58.1 21.6 %collective-permute-start.6 = (bf16[1,2,36864]{2,1,0:T(2,128)(2,1)S(1)}, bf16[1,2,36864]{2,1,0:T(2,128)(2,1)S(1)}, u32[]{:S(2)}, u32[]{:S(2)}) collective-permute-start(bf16[1,2,36864]{2,1,0:T(2,128)(2,1)S(1)} %get-tuple-element.14), channel_id=1, source_target_pairs={{0,7},{1,6},{2,5},{3,4},{4,3},{5,2},{6,1},{7,0},{8,15},{9,14},{10,... | collective-permute-start | bytes 442376 | tf_op jit(solution)/shard_map/ppermute | solution.py:65
  63.7 17.8 %collective-permute-start.7 = (bf16[1,2,36864]{2,1,0:T(2,128)(2,1)S(1)}, bf16[1,2,36864]{2,1,0:T(2,128)(2,1)S(1)}, u32[]{:S(2)}, u32[]{:S(2)}) collective-permute-start(bf16[1,2,36864]{2,1,0:T(2,128)(2,1)S(1)} %get-tuple-element.13), channel_id=1, source_target_pairs={{0,8},{1,9},{2,10},{3,11},{4,12},{5,13},{6,14},{7,15},{8,0},{9,1},... | collective-permute-start | bytes 442376 | tf_op jit(solution)/shard_map/ppermute | solution.py:65
  64.9 28.3 %collective-permute-start.8 = (bf16[1,2,36864]{2,1,0:T(2,128)(2,1)S(1)}, bf16[1,2,36864]{2,1,0:T(2,128)(2,1)S(1)}, u32[]{:S(2)}, u32[]{:S(2)}) collective-permute-start(bf16[1,2,36864]{2,1,0:T(2,128)(2,1)S(1)} %get-tuple-element.12), channel_id=1, source_target_pairs={{0,9},{1,8},{2,11},{3,10},{4,13},{5,12},{6,15},{7,14},{8,1},{9,0},... | collective-permute-start | bytes 442376 | tf_op jit(solution)/shard_map/ppermute | solution.py:65
  67.6 28.7 %collective-permute-start.9 = (bf16[1,2,36864]{2,1,0:T(2,128)(2,1)S(1)}, bf16[1,2,36864]{2,1,0:T(2,128)(2,1)S(1)}, u32[]{:S(2)}, u32[]{:S(2)}) collective-permute-start(bf16[1,2,36864]{2,1,0:T(2,128)(2,1)S(1)} %get-tuple-element.11), channel_id=1, source_target_pairs={{0,10},{1,11},{2,8},{3,9},{4,14},{5,15},{6,12},{7,13},{8,2},{9,3},... | collective-permute-start | bytes 442376 | tf_op jit(solution)/shard_map/ppermute | solution.py:65
  78.8 23.9 %collective-permute-start.10 = (bf16[1,2,36864]{2,1,0:T(2,128)(2,1)S(1)}, bf16[1,2,36864]{2,1,0:T(2,128)(2,1)S(1)}, u32[]{:S(2)}, u32[]{:S(2)}) collective-permute-start(bf16[1,2,36864]{2,1,0:T(2,128)(2,1)S(1)} %get-tuple-element.10), channel_id=1, source_target_pairs={{0,11},{1,10},{2,9},{3,8},{4,15},{5,14},{6,13},{7,12},{8,3},{9,2},... | collective-permute-start | bytes 442376 | tf_op jit(solution)/shard_map/ppermute | solution.py:65
  79.7 30.9 %collective-permute-start.11 = (bf16[1,2,36864]{2,1,0:T(2,128)(2,1)S(1)}, bf16[1,2,36864]{2,1,0:T(2,128)(2,1)S(1)}, u32[]{:S(2)}, u32[]{:S(2)}) collective-permute-start(bf16[1,2,36864]{2,1,0:T(2,128)(2,1)S(1)} %get-tuple-element.9), channel_id=1, source_target_pairs={{0,12},{1,13},{2,14},{3,15},{4,8},{5,9},{6,10},{7,11},{8,4},{9,5},... | collective-permute-start | bytes 442376 | tf_op jit(solution)/shard_map/ppermute | solution.py:65
  81.5 33.1 %collective-permute-start.12 = (bf16[1,2,36864]{2,1,0:T(2,128)(2,1)S(1)}, bf16[1,2,36864]{2,1,0:T(2,128)(2,1)S(1)}, u32[]{:S(2)}, u32[]{:S(2)}) collective-permute-start(bf16[1,2,36864]{2,1,0:T(2,128)(2,1)S(1)} %get-tuple-element.8), channel_id=1, source_target_pairs={{0,13},{1,12},{2,15},{3,14},{4,9},{5,8},{6,11},{7,10},{8,5},{9,4},... | collective-permute-start | bytes 442376 | tf_op jit(solution)/shard_map/ppermute | solution.py:65
  93.2 24.9 %collective-permute-start.13 = (bf16[1,2,36864]{2,1,0:T(2,128)(2,1)S(1)}, bf16[1,2,36864]{2,1,0:T(2,128)(2,1)S(1)}, u32[]{:S(2)}, u32[]{:S(2)}) collective-permute-start(bf16[1,2,36864]{2,1,0:T(2,128)(2,1)S(1)} %get-tuple-element.7), channel_id=1, source_target_pairs={{0,14},{1,15},{2,12},{3,13},{4,10},{5,11},{6,8},{7,9},{8,6},{9,7},... | collective-permute-start | bytes 442376 | tf_op jit(solution)/shard_map/ppermute | solution.py:65
  96.3 67.7 %collective-permute-start.14 = (bf16[1,2,36864]{2,1,0:T(2,128)(2,1)S(1)}, bf16[1,2,36864]{2,1,0:T(2,128)(2,1)S(1)}, u32[]{:S(2)}, u32[]{:S(2)}) collective-permute-start(bf16[1,2,36864]{2,1,0:T(2,128)(2,1)S(1)} %get-tuple-element.6), channel_id=1, source_target_pairs={{0,15},{1,14},{2,13},{3,12},{4,11},{5,10},{6,9},{7,8},{8,7},{9,6},... | collective-permute-start | bytes 442376 | tf_op jit(solution)/shard_map/ppermute | solution.py:65
  117.9 116.2 %reduce-scatter.2.cloned.1.call-start = ((), (), s32[]{:S(2)}) async-start(), calls=%async_computation.5 | async-start | bytes 6881280 | tf_op jit(solution)/shard_map/reduce_scatter | solution.py:96
  175.9 25.5 %copy-start.3 = (bf16[2048,576]{1,0:T(8,128)(2,1)}, bf16[2048,576]{1,0:T(8,128)(2,1)S(1)}, u32[]{:S(2)}) copy-start(bf16[2048,576]{1,0:T(8,128)(2,1)S(1)} %reshape.239) | copy-start | bytes 7077892
  237.3 6.7 %copy-start.4 = (bf16[2048,576]{1,0:T(8,128)(2,1)S(1)}, bf16[2048,576]{1,0:T(8,128)(2,1)}, u32[]{:S(2)}) copy-start(bf16[2048,576]{1,0:T(8,128)(2,1)} %copy-done.3) | copy-start | bytes 7077892
  237.3 48.6 %all-to-all-start.2 = ((bf16[16,10,3584]{2,1,0:T(8,128)(2,1)}), bf16[16,10,3584]{2,1,0:T(8,128)(2,1)}, u32[]{:S(2)}, u32[]{:S(2)}) async-start(bf16[16,10,3584]{2,1,0:T(8,128)(2,1)} %reshape.244), calls=%async_computation.3 | async-start | bytes 3670016 | tf_op jit(solution)/shard_map/all_to_all | solution.py:102
  (3 other events, 9.1 us)
Sparse Core Ops, SparseCore 0:
  118.0 33.3 all-gather.1
  164.2 58.6 reduce-scatter.1
